TPU v7x, 32 devices: a whole 2x2x4 slice. The times are simulated.
32 devices in a mesh: rows: 4 (over y, core), cols: 8 (over z, x).
Axes of the slice: x: 2, y: 2, z: 4, core: 2. Of those that a mesh axis runs over, the one named last changes fastest.
Arguments:
- costs: bfloat16 [4, 8, 24, 256, 256], P('rows', 'cols'), may hold values from -210 to 8
- block_rows: int32 [4, 8, 24], P('rows', 'cols'), may hold values from 0 to 7, as said below
- block_cols: int32 [4, 8, 24], P('rows', 'cols'), may hold values from 0 to 63, as said below
- live: int32 [4, 8], P('rows', 'cols'), may hold values from 16 to 24, as said below
- log_source: float32 [8192], P('rows'), may hold values from -6 to 6
- log_target: float32 [131072], P('cols'), may hold values from -6 to 6
Outputs:
- source_potential: float32 [8192], P('rows')
- target_potential: float32 [131072], P('cols')
Inputs may be any that keep to these rules, and one draw needn't show every extreme that they name: `block_rows`: row blocks are local to a device's 8 blocks of source cells. `block_cols`: column blocks are local to a device's 64 blocks of target cells. Every source cell and every target cell lies in some live block. `live`: live counts differ from device to device; some device uses all 24 slots.
All inputs are finite; a program needn't handle non-finite values.
Results may differ from a plain program's by a relative error of at most 0.0003.
Values sent between devices are 32-bit elements; how exact they have to be, the bound alone decides.
A program may use at most 64 MiB of HBM per device.

v0:
```python
import functools

import jax
import jax.numpy as jnp
from jax import lax
from jax.experimental import pallas as pl
from jax.experimental.pallas import tpu as pltpu
from jax.sharding import PartitionSpec as P

ITERS = 3
NEG = -1e30
LOG2E = 1.4426950408889634
LN2 = 0.6931471805599453
LANES = 128
GROUP = 8
MESH = pl.DeviceIdType.MESH


def log2(x):
    return jnp.log(x) * LOG2E


def kernel(
    n_rows, n_cols,
    brows, bcols, live, costs, log_src, log_tgt,
    src_out, lse_out, ids_out,
    tiles, tiles_s, tiles_t, rid, cid, slot_top, slot_tot, part_src, part_tgt, columns, src_col, piece, lt_piece,
    cid_all, src_buf, tgt_buf,
    load_sem, cid_send, cid_recv, src_send, src_recv, tgt_send, tgt_recv,
):
    slots, bs, _ = tiles.shape
    halves = bs // LANES
    row_blocks = part_src.shape[1]
    my_r = lax.axis_index("rows")
    my_c = lax.axis_index("cols")

    barrier = pltpu.get_barrier_semaphore()
    for k in range(1, n_rows):
        pl.semaphore_signal(barrier, inc=1, device_id=(lax.rem(my_r + k, n_rows), my_c), device_id_type=MESH)
    for k in range(1, n_cols):
        pl.semaphore_signal(barrier, inc=1, device_id=(my_r, lax.rem(my_c + k, n_cols)), device_id_type=MESH)

    loads = []
    for c in range(slots // GROUP):
        part = pl.ds(c * GROUP, GROUP)
        loads.append(pltpu.make_async_copy(costs.at[part], tiles.at[part], load_sem.at[c]))
        loads[-1].start()

    count = live[0]
    for t in range(slots):
        okay = t < count
        rid[t : t + 1, :] = jnp.full((1, LANES), jnp.where(okay, brows[t], -1), jnp.int32)
        cid[t : t + 1, :] = jnp.full((1, LANES), jnp.where(okay, bcols[t], -1), jnp.int32)
    wide_cid = cid[...]
    cid_all[pl.ds(my_r, 1)] = wide_cid[None]

    def send(k, along, src, dst, send_sem, recv_sem):
        if along == "rows":
            peer = (lax.rem(my_r + k, n_rows), my_c)
        else:
            peer = (my_r, lax.rem(my_c + k, n_cols))
        return pltpu.make_async_remote_copy(
            src_ref=src, dst_ref=dst, send_sem=send_sem, recv_sem=recv_sem,
            device_id=peer, device_id_type=MESH)

    def exchange(along, n, me, src, buf, send_sem, recv_sem):
        outs = [send(k, along, src, buf.at[me], send_sem.at[k], recv_sem.at[k]) for k in range(1, n)]
        for copy in outs:
            copy.start()
        return outs

    def arrived(along, n, me, src, buf, send_sem, recv_sem):
        for k in range(1, n):
            frm = lax.rem(me + n - k, n)
            send(k, along, src, buf.at[frm], send_sem.at[k], recv_sem.at[k]).wait_recv()

    def group_lse(g, h, col, tile):
        lanes = slice(h * LANES, (h + 1) * LANES)
        tops, tots = [], []
        for i in range(GROUP):
            t = g * GROUP + i
            column = col(t, i)
            score = -tile[t, :, lanes] if column is None else column - tile[t, :, lanes]
            top = jnp.max(score, axis=0, keepdims=True)
            tops.append(top)
            tots.append(jnp.sum(jnp.exp2(score - top), axis=0, keepdims=True))
        at = pl.ds(pl.multiple_of(g * GROUP, GROUP), GROUP)
        slot_top[h, at, :] = jnp.concatenate(tops, axis=0)
        slot_tot[h, at, :] = jnp.concatenate(tots, axis=0)

    def slot_lse(h, ids):
        return jnp.where(ids >= 0, slot_top[h] + log2(slot_tot[h]), NEG)

    def as_column(row):
        return jnp.concatenate(
            [jnp.broadcast_to(row[:, h * LANES : (h + 1) * LANES], (LANES, LANES)).T for h in range(halves)], axis=0)

    eye = (lax.broadcasted_iota(jnp.int32, (bs, bs), 0) == lax.broadcasted_iota(jnp.int32, (bs, bs), 1))
    eye = eye.astype(jnp.float32).astype(jnp.bfloat16)
    for c in range(slots // GROUP):
        loads[c].wait()

        def turn(t, _):
            tile = tiles[t]
            turned = lax.dot_general(eye, tile, (((1,), (1,)), ((), ())), preferred_element_type=jnp.float32)
            tiles_t[t] = turned * LOG2E
            tiles_s[t] = tile.astype(jnp.float32) * LOG2E
            return 0

        lax.fori_loop(c * GROUP, (c + 1) * GROUP, turn, 0, unroll=2)
        for h in range(halves):
            group_lse(c, h, lambda t, i: None, tiles_t)

    pl.semaphore_wait(barrier, n_rows + n_cols - 2)
    cid_copies = exchange("rows", n_rows, my_r, cid, cid_all, cid_send, cid_recv)

    for t in range(slots):
        col_at = bcols[t] * halves
        for h in range(halves):
            lt_piece[h, t : t + 1, :] = log_tgt[pl.ds(col_at + h, 1), :] * LOG2E
    waits = list(cid_copies)
    block_of = lax.broadcasted_iota(jnp.int32, (row_blocks, LANES), 0)
    for sweep in range(ITERS):
        mine = []
        for h in range(halves):
            if sweep:
                def row_group(g, _):
                    at = pl.ds(pl.multiple_of(g * GROUP, GROUP), GROUP)
                    rows = jnp.concatenate([piece[k, at, :] for k in range(halves)], axis=1)

                    def column(t, i):
                        if h:
                            return columns[t]
                        made = as_column(rows[i : i + 1])
                        columns[t] = made
                        return made

                    group_lse(g, h, column, tiles_t)
                    return 0

                lax.fori_loop(0, slots // GROUP, row_group, 0)
            found = slot_lse(h, rid[...])
            masked = [jnp.where(block_of == rid[t : t + 1, :], found[t : t + 1, :], NEG) for t in range(slots)]
            top = functools.reduce(jnp.maximum, masked)
            total = functools.reduce(jnp.add, [jnp.exp2(value - top) for value in masked])
            part_src[h] = top + log2(total)
            mine += exchange("cols", n_cols, my_c, part_src.at[h], src_buf.at[sweep, h], src_send.at[sweep, h], src_recv.at[sweep, h])
            src_buf[sweep, h, pl.ds(my_c, 1)] = part_src[h][None]
        sources = []
        for h in range(halves):
            arrived("cols", n_cols, my_c, part_src.at[h], src_buf.at[sweep, h], src_send.at[sweep, h], src_recv.at[sweep, h])
            theirs = [src_buf[sweep, h, k] for k in range(n_cols)]
            top = functools.reduce(jnp.maximum, theirs)
            total = functools.reduce(jnp.add, [jnp.exp2(value - top) for value in theirs])
            source = log_src[pl.ds(h, row_blocks, stride=halves), :] * LOG2E - (top + log2(total))
            sources.append(source)
            for b in range(row_blocks):
                src_col[b, h * LANES : (h + 1) * LANES, :] = jnp.broadcast_to(source[b : b + 1, :], (LANES, LANES)).T
        for copy in mine:
            copy.wait_send()
        if sweep == 0:
            arrived("rows", n_rows, my_r, cid, cid_all, cid_send, cid_recv)
        mine = []
        for h in range(halves):
            def col_group(g, _):
                group_lse(g, h, lambda t, i: src_col[brows[t]], tiles_s)
                return 0

            lax.fori_loop(0, slots // GROUP, col_group, 0)
            part_tgt[h] = slot_lse(h, cid[...])
            mine += exchange("rows", n_rows, my_r, part_tgt.at[h], tgt_buf.at[sweep, h], tgt_send.at[sweep, h], tgt_recv.at[sweep, h])
            tgt_buf[sweep, h, pl.ds(my_r, 1)] = part_tgt[h][None]
        for h in range(halves):
            arrived("rows", n_rows, my_r, part_tgt.at[h], tgt_buf.at[sweep, h], tgt_send.at[sweep, h], tgt_recv.at[sweep, h])
            lanes = slice(h * LANES, (h + 1) * LANES)
            if sweep == ITERS - 1:
                for r in range(n_rows):
                    lse_out[r * slots : (r + 1) * slots, lanes] = tgt_buf[sweep, h, r]
                    ids_out[r * slots : (r + 1) * slots, :] = cid_all[r]
                src_out[:, lanes] = sources[h] * LN2
                continue
            ids = cid[...]

            def each(g):
                at = pl.ds(pl.multiple_of(g * GROUP, GROUP), GROUP)
                for r in range(n_rows):
                    theirs, values = cid_all[r, at, :], tgt_buf[sweep, h, r, at, :]
                    for i in range(GROUP):
                        yield jnp.where(ids == theirs[i : i + 1], values[i : i + 1], NEG)

            def top_of(g, top):
                return functools.reduce(jnp.maximum, each(g), top)

            top = lax.fori_loop(0, slots // GROUP, top_of, jnp.full(ids.shape, NEG, jnp.float32))

            def total_of(g, total):
                return functools.reduce(lambda so_far, value: so_far + jnp.exp2(value - top), each(g), total)

            total = lax.fori_loop(0, slots // GROUP, total_of, jnp.zeros(ids.shape, jnp.float32))
            piece[h] = jnp.where(ids >= 0, lt_piece[h] - (top + log2(total)), 0.0)
        for copy in mine:
            copy.wait_send()
    for copy in waits:
        copy.wait_send()


def final_kernel(source, lse, ids, log_tgt, src_out, tgt_out, top_buf):
    found, bs = lse.shape
    halves = bs // LANES
    blocks = tgt_out.shape[0] // halves
    exact = functools.partial(jnp.dot, preferred_element_type=jnp.float32, precision=lax.Precision.HIGHEST)
    per = 16 if blocks % 16 == 0 else blocks
    for b in range(0, blocks, per):
        block = lax.broadcasted_iota(jnp.int32, (per, LANES), 0) + b

        def top_of(g, top):
            at = pl.ds(pl.multiple_of(g * GROUP, GROUP), GROUP)
            theirs, values = ids[at, :], lse[at, :]
            for i in range(GROUP):
                here = jnp.concatenate([block == theirs[i : i + 1]] * halves, axis=1)
                top = jnp.maximum(top, jnp.where(here, values[i : i + 1], NEG))
            return top

        top_buf[b : b + per, :] = lax.fori_loop(
            0, found // GROUP, top_of, jnp.full((per, bs), NEG, jnp.float32), unroll=3 if found % (3 * GROUP) == 0 else 2)
    top = top_buf[...]
    names = ids[...].astype(jnp.float32)
    back = (names[:, 0:1] == lax.broadcasted_iota(jnp.int32, (found, blocks), 1).astype(jnp.float32)).astype(jnp.float32)
    into = (names.T[0:1, :] == lax.broadcasted_iota(jnp.int32, (blocks, found), 0).astype(jnp.float32)).astype(jnp.float32)
    total = exact(into, jnp.exp2(lse[...] - exact(back, top)))
    found_lse = top * LN2 + jnp.log(total)
    for h in range(halves):
        rows = pl.ds(h, blocks, stride=halves)
        tgt_out[rows, :] = log_tgt[rows, :] - found_lse[:, h * LANES : (h + 1) * LANES]
        src_out[pl.ds(h, source.shape[0], stride=halves), :] = source[:, h * LANES : (h + 1) * LANES]


def per_device(n_rows, n_cols, costs, block_rows, block_cols, live, log_source, log_target):
    tiles = costs[0, 0]
    slots, bs, _ = tiles.shape
    src_rows = log_source.shape[0] // LANES
    tgt_rows = log_target.shape[0] // LANES
    row_blocks = log_source.shape[0] // bs
    f32 = jnp.float32
    halves = bs // LANES
    dma = pltpu.SemaphoreType.DMA
    smem = pl.BlockSpec(memory_space=pltpu.SMEM)
    vmem = pl.BlockSpec(memory_space=pltpu.VMEM)
    found = n_rows * slots
    source, lse, ids = pl.pallas_call(
        functools.partial(kernel, n_rows, n_cols),
        out_shape=(
            jax.ShapeDtypeStruct((row_blocks, bs), f32),
            jax.ShapeDtypeStruct((found, bs), f32),
            jax.ShapeDtypeStruct((found, LANES), jnp.int32),
        ),
        in_specs=[smem, smem, smem, pl.BlockSpec(memory_space=pl.ANY), vmem, vmem],
        out_specs=(vmem, vmem, vmem),
        scratch_shapes=[
            pltpu.VMEM((slots, bs, bs), tiles.dtype),
            pltpu.VMEM((slots, bs, bs), f32),
            pltpu.VMEM((slots, bs, bs), f32),
            pltpu.VMEM((slots, LANES), jnp.int32),
            pltpu.VMEM((slots, LANES), jnp.int32),
            pltpu.VMEM((halves, slots, LANES), f32),
            pltpu.VMEM((halves, slots, LANES), f32),
            pltpu.VMEM((halves, row_blocks, LANES), f32),
            pltpu.VMEM((halves, slots, LANES), f32),
            pltpu.VMEM((slots, bs, LANES), f32),
            pltpu.VMEM((row_blocks, bs, LANES), f32),
            pltpu.VMEM((halves, slots, LANES), f32),
            pltpu.VMEM((halves, slots, LANES), f32),
            pltpu.VMEM((n_rows, slots, LANES), jnp.int32),
            pltpu.VMEM((ITERS, halves, n_cols, row_blocks, LANES), f32),
            pltpu.VMEM((ITERS, halves, n_rows, slots, LANES), f32),
            dma((slots // GROUP,)),
            dma((n_rows,)), dma((n_rows,)),
            dma((ITERS, halves, n_cols)), dma((ITERS, halves, n_cols)),
            dma((ITERS, halves, n_rows)), dma((ITERS, halves, n_rows)),
        ],
        compiler_params=pltpu.CompilerParams(collective_id=0, has_side_effects=True),
    )(
        block_rows.reshape(-1), block_cols.reshape(-1), live.reshape(-1), tiles,
        log_source.reshape(src_rows, LANES), log_target.reshape(tgt_rows, LANES),
    )
    source, target = pl.pallas_call(
        final_kernel,
        out_shape=(jax.ShapeDtypeStruct((src_rows, LANES), f32), jax.ShapeDtypeStruct((tgt_rows, LANES), f32)),
        in_specs=[vmem] * 4,
        out_specs=(vmem, vmem),
        scratch_shapes=[pltpu.VMEM((tgt_rows * LANES // bs, bs), f32)],
    )(source, lse, ids, log_target.reshape(tgt_rows, LANES))
    return source.reshape(-1), target.reshape(-1)


def solution(mesh):
    in_specs = (
        P("rows", "cols", None, None, None),
        P("rows", "cols", None),
        P("rows", "cols", None),
        P("rows", "cols"),
        P("rows"),
        P("cols"),
    )
    out_specs = (P("rows"), P("cols"))
    body = functools.partial(per_device, mesh.shape["rows"], mesh.shape["cols"])
    return jax.shard_map(body, mesh=mesh, in_specs=in_specs, out_specs=out_specs, check_vma=False)
```

profile of v0, /device:TPU:0, one launch (start us, length us, event | category | flops | bytes accessed | tf_op | source)
XLA Modules:
  0.0 49.0 jit_solution(4220222941400859727)
XLA Ops:
  1.3 45.0 %shard_map.77 = (f32[8,256]{1,0:T(8,128)}, f32[96,256]{1,0:T(8,128)}, s32[96,128]{1,0:T(8,128)}) custom-call(s32[24]{0:T(128)} %bitcast.13, s32[24]{0:T(128)} %bitcast.14, s32[1]{0:T(128)} %bitcast.8.live, bf16[24,256,256]{2,1,0:T(8,128)(2,1)} %bitcast.9, f32[16,128]{1,0:T(8,128)} %bitcast.12, f32[128,128]{1,0:T(8,128)} %bitcast.10), custom_call_target="tpu_custom_call" | custom-call | tf_op jit(solution)/shard_map/pallas_call | solution.py:250
  46.3 2.7 %shard_map.78 = (f32[16,128]{1,0:T(8,128)}, f32[128,128]{1,0:T(8,128)}) custom-call(f32[8,256]{1,0:T(8,128)} %get-tuple-element.7.source, f32[96,256]{1,0:T(8,128)} %get-tuple-element.8.lse, s32[96,128]{1,0:T(8,128)} %get-tuple-element.9.ids, f32[128,128]{1,0:T(8,128)} %bitcast.11), custom_call_target="tpu_custom_call" | custom-call | tf_op jit(solution)/shard_map/pallas_call | solution.py:286
where the time goes:
time: 49.2 us; the launch traced here: 49 us
  Pallas kernels  47.7 us (97%)
  between operations  1.28 us (3%)
    pallas_call x1, Pallas kernels, per_device(): pl.pallas_call(functools.partial(kernel, n_rows, n_cols), out_shape=(jax....  45 us
    pallas_call x1, Pallas kernels, per_device(): pl.pallas_call(final_kernel, out_shape=(jax.ShapeDtypeStruct((src_rows, L...  2.68 us

commit v1 on v0

v1 whole, which is shorter than its diff:
```python
import functools

import jax
import jax.numpy as jnp
from jax import lax
from jax.experimental import pallas as pl
from jax.experimental.pallas import tpu as pltpu
from jax.sharding import PartitionSpec as P

ITERS = 3
NEG = -1e30
LOG2E = 1.4426950408889634
LN2 = 0.6931471805599453
LANES = 128
GROUP = 8
HEAD = 28.0
SCALE = 66.0
MESH = pl.DeviceIdType.MESH


def log2(x):
    return jnp.log(x) * LOG2E


def split_peer(me, k, n):
    if n & (n - 1):
        return lax.rem(me + k, n), lax.rem(me + n - k, n)
    other = me
    bit = 1
    while bit <= k:
        if k & bit:
            other = other + bit - 2 * bit * lax.rem(lax.div(me, bit), 2)
        bit *= 2
    return other, other


def kernel(
    n_rows, n_cols,
    brows, bcols, live, costs, log_src, log_tgt,
    src_out, lse_out, ids_out,
    tiles, tiles_s, tiles_t, rid, cid, base, slot_tot, part_src, part_tgt, src_row, columns, weight, lt_piece,
    cid_all, src_buf, tgt_buf,
    load_sem, cid_send, cid_recv, src_send, src_recv, tgt_send, tgt_recv,
):
    slots, bs, _ = tiles.shape
    halves = bs // LANES
    row_blocks = src_row.shape[0]
    my_r = lax.axis_index("rows")
    my_c = lax.axis_index("cols")

    barrier = pltpu.get_barrier_semaphore()
    for k in range(n_cols - 1, 0, -1):
        pl.semaphore_signal(barrier, inc=1, device_id=(my_r, split_peer(my_c, k, n_cols)[0]), device_id_type=MESH)
    for k in range(n_rows - 1, 0, -1):
        pl.semaphore_signal(barrier, inc=1, device_id=(split_peer(my_r, k, n_rows)[0], my_c), device_id_type=MESH)

    loads = []
    for c in range(slots // GROUP):
        part = pl.ds(c * GROUP, GROUP)
        loads.append(pltpu.make_async_copy(costs.at[part], tiles.at[part], load_sem.at[c]))
        loads[-1].start()

    count = live[0]
    for t in range(slots):
        okay = t < count
        rid[t : t + 1, :] = jnp.full((1, bs), jnp.where(okay, brows[t], -1), jnp.int32)
        cid[t : t + 1, :] = jnp.full((1, bs), jnp.where(okay, bcols[t], -1), jnp.int32)
    cid_all[pl.ds(my_r, 1)] = cid[:, :LANES][None]

    def exchange(along, n, me, src, buf, send_sem, recv_sem):
        copies = []
        for k in range(n - 1, 0, -1):
            to = split_peer(me, k, n)[0]
            peer = (to, my_c) if along == "rows" else (my_r, to)
            copies.append(pltpu.make_async_remote_copy(
                src_ref=src, dst_ref=buf.at[me], send_sem=send_sem.at[k], recv_sem=recv_sem.at[k],
                device_id=peer, device_id_type=MESH))
            copies[-1].start()
        return copies

    def arrived(along, n, me, src, buf, send_sem, recv_sem):
        for k in range(1, n):
            to, frm = split_peer(me, k, n)
            peer = (to, my_c) if along == "rows" else (my_r, to)
            pltpu.make_async_remote_copy(
                src_ref=src, dst_ref=buf.at[frm], send_sem=send_sem.at[k], recv_sem=recv_sem.at[k],
                device_id=peer, device_id_type=MESH).wait_recv()

    def as_column(row):
        return jnp.concatenate(
            [jnp.broadcast_to(row[:, h * LANES : (h + 1) * LANES], (LANES, LANES)).T for h in range(halves)], axis=0)

    def groups(body):
        def step(g, _):
            body(g, pl.ds(pl.multiple_of(g * GROUP, GROUP), GROUP))
            return 0

        lax.fori_loop(0, slots // GROUP, step, 0)

    cuts = [slice(h * LANES, (h + 1) * LANES) for h in range(halves)]
    eye = (lax.broadcasted_iota(jnp.int32, (bs, bs), 0) == lax.broadcasted_iota(jnp.int32, (bs, bs), 1))
    eye = eye.astype(jnp.float32).astype(jnp.bfloat16)
    for c in range(slots // GROUP):
        loads[c].wait()

        def turn(t, _):
            tile = tiles[t]
            turned = lax.dot_general(eye, tile, (((1,), (1,)), ((), ())), preferred_element_type=jnp.float32)
            tiles_t[t] = turned * LOG2E
            tiles_s[t] = tile.astype(jnp.float32) * LOG2E
            return 0

        lax.fori_loop(c * GROUP, (c + 1) * GROUP, turn, 0, unroll=2)
        at = slice(c * GROUP, (c + 1) * GROUP)
        for lanes in cuts:
            lows, tots = [], []
            for i in range(GROUP):
                cost = tiles_t[c * GROUP + i, :, lanes]
                low = jnp.min(cost, axis=0, keepdims=True)
                lows.append(low)
                tots.append(jnp.sum(jnp.exp2(low - cost), axis=0, keepdims=True))
            base[at, lanes] = -jnp.concatenate(lows, axis=0)
            slot_tot[at, lanes] = jnp.concatenate(tots, axis=0)

    block_of = lax.broadcasted_iota(jnp.int32, (row_blocks, bs), 0)
    found = base[...] + log2(slot_tot[...])
    masked = [jnp.where(block_of == rid[t : t + 1, :], found[t : t + 1, :], NEG) for t in range(slots)]
    top = functools.reduce(jnp.maximum, masked)
    total = functools.reduce(jnp.add, [jnp.exp2(value - top) for value in masked])
    part_src[0] = top + log2(total)
    src_buf[0, pl.ds(my_c, 1)] = part_src[0][None]

    pl.semaphore_wait(barrier, n_rows + n_cols - 2)

    def send_src(sweep):
        return exchange("cols", n_cols, my_c, part_src.at[sweep], src_buf.at[sweep], src_send.at[sweep], src_recv.at[sweep])

    def get_src(sweep):
        arrived("cols", n_cols, my_c, part_src.at[sweep], src_buf.at[sweep], src_send.at[sweep], src_recv.at[sweep])
        return [src_buf[sweep, k] for k in range(n_cols)]

    def send_tgt(sweep):
        return exchange("rows", n_rows, my_r, part_tgt.at[sweep], tgt_buf.at[sweep], tgt_send.at[sweep], tgt_recv.at[sweep])

    def get_tgt(sweep):
        arrived("rows", n_rows, my_r, part_tgt.at[sweep], tgt_buf.at[sweep], tgt_send.at[sweep], tgt_recv.at[sweep])

    waits = send_src(0)
    waits += exchange("rows", n_rows, my_r, cid_all.at[my_r], cid_all, cid_send, cid_recv)

    for t in range(slots):
        col_at = bcols[t] * halves
        for h, lanes in enumerate(cuts):
            lt_piece[t : t + 1, lanes] = log_tgt[pl.ds(col_at + h, 1), :] * LOG2E
    log_a = jnp.concatenate([log_src[pl.ds(h, row_blocks, stride=halves), :] for h in range(halves)], axis=1) * LOG2E

    theirs = get_src(0)
    top = functools.reduce(jnp.maximum, theirs)
    total = functools.reduce(jnp.add, [jnp.exp2(value - top) for value in theirs])
    first = log_a - (top + log2(total))
    src_row[...] = first

    def put_columns(values):
        for b in range(row_blocks):
            columns[b] = as_column(values[b : b + 1, :])

    put_columns(first)

    def first_col(g, at):
        for lanes in cuts:
            tops, tots = [], []
            for i in range(GROUP):
                t = g * GROUP + i
                score = columns[brows[t]] - tiles_s[t, :, lanes]
                top = jnp.max(score, axis=0, keepdims=True) - HEAD
                entry = jnp.exp2(score - top)
                tiles_s[t, :, lanes] = entry
                tops.append(top)
                tots.append(jnp.sum(entry, axis=0, keepdims=True))
            base[at, lanes] = jnp.concatenate(tops, axis=0)
            slot_tot[at, lanes] = jnp.concatenate(tots, axis=0)

    groups(first_col)
    alive = cid[...] >= 0
    part_tgt[0] = jnp.where(alive, base[...] + log2(slot_tot[...]), NEG)
    tgt_buf[0, pl.ds(my_r, 1)] = part_tgt[0][None]
    waits += send_tgt(0)

    def first_turned(g, at):
        bases = base[at, :]
        for i in range(GROUP):
            t = g * GROUP + i
            down = as_column(bases[i : i + 1])
            row = src_row[pl.ds(brows[t], 1), :]
            for lanes in cuts:
                tiles_t[t, :, lanes] = jnp.exp2((row[:, lanes] - tiles_t[t, :, lanes]) - down)

    groups(first_turned)
    arrived("rows", n_rows, my_r, cid_all.at[my_r], cid_all, cid_send, cid_recv)
    get_tgt(0)

    def candidates(sweep, lanes, fill):
        ids = cid[:, :LANES]

        def each(g):
            at = pl.ds(pl.multiple_of(g * GROUP, GROUP), GROUP)
            for r in range(n_rows):
                theirs, values = cid_all[r, at, :], tgt_buf[sweep, r, at, lanes]
                for i in range(GROUP):
                    yield jnp.where(ids == theirs[i : i + 1], values[i : i + 1], fill)

        def fold(op, start):
            return lax.fori_loop(0, slots // GROUP, lambda g, so_far: functools.reduce(op, each(g), so_far), start)

        return fold

    for lanes in cuts:
        fold = candidates(0, lanes, NEG)
        top = fold(jnp.maximum, jnp.full((slots, LANES), NEG, jnp.float32))
        total = fold(lambda so_far, value: so_far + jnp.exp2(value - top), jnp.zeros((slots, LANES), jnp.float32))
        gain = lt_piece[:, lanes] - (top + log2(total)) + (base[:, lanes] + SCALE)
        weight[:, lanes] = jnp.where(cid[:, lanes] >= 0, jnp.exp2(gain), 0.0)
    anchor = weight[...]
    goal_a = jnp.exp2(log_a + SCALE)

    for sweep in range(1, ITERS):
        def row_sums(g, at):
            rows = weight[at, :]
            sums = []
            for i in range(GROUP):
                t = g * GROUP + i
                down = as_column(rows[i : i + 1])
                sums.append(jnp.concatenate(
                    [jnp.sum(tiles_t[t, :, lanes] * down, axis=0, keepdims=True) for lanes in cuts], axis=1))
            slot_tot[at, :] = jnp.concatenate(sums, axis=0)

        groups(row_sums)
        part_src[sweep] = functools.reduce(
            jnp.add, [jnp.where(block_of == rid[t : t + 1, :], slot_tot[t : t + 1, :], 0.0) for t in range(slots)])
        src_buf[sweep, pl.ds(my_c, 1)] = part_src[sweep][None]
        waits += send_src(sweep)
        scaling = goal_a / functools.reduce(jnp.add, get_src(sweep))
        put_columns(scaling)

        def col_sums(g, at):
            sums = []
            for i in range(GROUP):
                t = g * GROUP + i
                down = columns[brows[t]]
                sums.append(jnp.concatenate(
                    [jnp.sum(tiles_s[t, :, lanes] * down, axis=0, keepdims=True) for lanes in cuts], axis=1))
            slot_tot[at, :] = jnp.concatenate(sums, axis=0)

        groups(col_sums)
        if sweep < ITERS - 1:
            part_tgt[sweep] = anchor * slot_tot[...]
        else:
            part_tgt[sweep] = jnp.where(alive, base[...] + log2(slot_tot[...]), NEG)
        tgt_buf[sweep, pl.ds(my_r, 1)] = part_tgt[sweep][None]
        waits += send_tgt(sweep)
        if sweep < ITERS - 1:
            goal_b = jnp.exp2(lt_piece[...] + SCALE)
        else:
            src_out[...] = (src_row[...] + log2(scaling)) * LN2
        get_tgt(sweep)
        if sweep == ITERS - 1:
            for r in range(n_rows):
                lse_out[r * slots : (r + 1) * slots, :] = tgt_buf[sweep, r]
                ids_out[r * slots : (r + 1) * slots, :] = cid_all[r]
            continue
        for lanes in cuts:
            total = candidates(sweep, lanes, 0.0)(jnp.add, jnp.zeros((slots, LANES), jnp.float32))
            weight[:, lanes] = jnp.where(
                cid[:, lanes] >= 0, anchor[:, lanes] * (goal_b[:, lanes] / total), 0.0)
    for copy in waits:
        copy.wait_send()


def final_kernel(source, lse, ids, log_tgt, src_out, tgt_out, top_buf):
    found, bs = lse.shape
    halves = bs // LANES
    blocks = tgt_out.shape[0] // halves
    exact = functools.partial(jnp.dot, preferred_element_type=jnp.float32, precision=lax.Precision.HIGHEST)
    per = 16 if blocks % 16 == 0 else blocks
    for b in range(0, blocks, per):
        block = lax.broadcasted_iota(jnp.int32, (per, LANES), 0) + b

        def top_of(g, top):
            at = pl.ds(pl.multiple_of(g * GROUP, GROUP), GROUP)
            theirs, values = ids[at, :], lse[at, :]
            for i in range(GROUP):
                here = jnp.concatenate([block == theirs[i : i + 1]] * halves, axis=1)
                top = jnp.maximum(top, jnp.where(here, values[i : i + 1], NEG))
            return top

        top_buf[b : b + per, :] = lax.fori_loop(
            0, found // GROUP, top_of, jnp.full((per, bs), NEG, jnp.float32), unroll=3 if found % (3 * GROUP) == 0 else 2)
    top = top_buf[...]
    names = ids[...].astype(jnp.float32)
    back = (names[:, 0:1] == lax.broadcasted_iota(jnp.int32, (found, blocks), 1).astype(jnp.float32)).astype(jnp.float32)
    into = (names.T[0:1, :] == lax.broadcasted_iota(jnp.int32, (blocks, found), 0).astype(jnp.float32)).astype(jnp.float32)
    total = exact(into, jnp.exp2(lse[...] - exact(back, top)))
    found_lse = top * LN2 + jnp.log(total)
    for h in range(halves):
        rows = pl.ds(h, blocks, stride=halves)
        tgt_out[rows, :] = log_tgt[rows, :] - found_lse[:, h * LANES : (h + 1) * LANES]
        src_out[pl.ds(h, source.shape[0], stride=halves), :] = source[:, h * LANES : (h + 1) * LANES]


def per_device(n_rows, n_cols, costs, block_rows, block_cols, live, log_source, log_target):
    tiles = costs[0, 0]
    slots, bs, _ = tiles.shape
    src_rows = log_source.shape[0] // LANES
    tgt_rows = log_target.shape[0] // LANES
    row_blocks = log_source.shape[0] // bs
    f32 = jnp.float32
    halves = bs // LANES
    dma = pltpu.SemaphoreType.DMA
    smem = pl.BlockSpec(memory_space=pltpu.SMEM)
    vmem = pl.BlockSpec(memory_space=pltpu.VMEM)
    found = n_rows * slots
    source, lse, ids = pl.pallas_call(
        functools.partial(kernel, n_rows, n_cols),
        out_shape=(
            jax.ShapeDtypeStruct((row_blocks, bs), f32),
            jax.ShapeDtypeStruct((found, bs), f32),
            jax.ShapeDtypeStruct((found, LANES), jnp.int32),
        ),
        in_specs=[smem, smem, smem, pl.BlockSpec(memory_space=pl.ANY), vmem, vmem],
        out_specs=(vmem, vmem, vmem),
        scratch_shapes=[
            pltpu.VMEM((slots, bs, bs), tiles.dtype),
            pltpu.VMEM((slots, bs, bs), f32),
            pltpu.VMEM((slots, bs, bs), f32),
            pltpu.VMEM((slots, bs), jnp.int32),
            pltpu.VMEM((slots, bs), jnp.int32),
            pltpu.VMEM((slots, bs), f32),
            pltpu.VMEM((slots, bs), f32),
            pltpu.VMEM((ITERS, row_blocks, bs), f32),
            pltpu.VMEM((ITERS, slots, bs), f32),
            pltpu.VMEM((row_blocks, bs), f32),
            pltpu.VMEM((row_blocks, bs, LANES), f32),
            pltpu.VMEM((slots, bs), f32),
            pltpu.VMEM((slots, bs), f32),
            pltpu.VMEM((n_rows, slots, LANES), jnp.int32),
            pltpu.VMEM((ITERS, n_cols, row_blocks, bs), f32),
            pltpu.VMEM((ITERS, n_rows, slots, bs), f32),
            dma((slots // GROUP,)),
            dma((n_rows,)), dma((n_rows,)),
            dma((ITERS, n_cols)), dma((ITERS, n_cols)),
            dma((ITERS, n_rows)), dma((ITERS, n_rows)),
        ],
        compiler_params=pltpu.CompilerParams(collective_id=0, has_side_effects=True),
    )(
        block_rows.reshape(-1), block_cols.reshape(-1), live.reshape(-1), tiles,
        log_source.reshape(src_rows, LANES), log_target.reshape(tgt_rows, LANES),
    )
    source, target = pl.pallas_call(
        final_kernel,
        out_shape=(jax.ShapeDtypeStruct((src_rows, LANES), f32), jax.ShapeDtypeStruct((tgt_rows, LANES), f32)),
        in_specs=[vmem] * 4,
        out_specs=(vmem, vmem),
        scratch_shapes=[pltpu.VMEM((tgt_rows * LANES // bs, bs), f32)],
    )(source, lse, ids, log_target.reshape(tgt_rows, LANES))
    return source.reshape(-1), target.reshape(-1)


def solution(mesh):
    in_specs = (
        P("rows", "cols", None, None, None),
        P("rows", "cols", None),
        P("rows", "cols", None),
        P("rows", "cols"),
        P("rows"),
        P("cols"),
    )
    out_specs = (P("rows"), P("cols"))
    body = functools.partial(per_device, mesh.shape["rows"], mesh.shape["cols"])
    return jax.shard_map(body, mesh=mesh, in_specs=in_specs, out_specs=out_specs, check_vma=False)
```

time: 49.2 us -> 45.2 us (0.919)
  Pallas kernels: 47.7 us -> 43.7 us
    pallas_call x1, Pallas kernels: 45 us -> 41 us  [per_device(): pl.pallas_call(functools.partial(kernel, n_rows, n_cols), out_shape=(jax....]
where the time goes in v1:
time: 45.2 us; the launch traced here: 45 us
  Pallas kernels  43.7 us (97%)
  between operations  1.28 us (3%)
    pallas_call x1, Pallas kernels, per_device(): pl.pallas_call(functools.partial(kernel, n_rows, n_cols), out_shape=(jax....  41 us
    pallas_call x1, Pallas kernels, per_device(): pl.pallas_call(final_kernel, out_shape=(jax.ShapeDtypeStruct((src_rows, L...  2.68 us

profile of v1, /device:TPU:0, one launch (start us, length us, event | category | flops | bytes accessed | tf_op | source)
XLA Modules:
  0.0 45.0 jit_solution(4169054731901370593)
XLA Ops:
  1.3 41.0 %shard_map.77 = (f32[8,256]{1,0:T(8,128)}, f32[96,256]{1,0:T(8,128)}, s32[96,128]{1,0:T(8,128)}) custom-call(s32[24]{0:T(128)} %bitcast.13, s32[24]{0:T(128)} %bitcast.14, s32[1]{0:T(128)} %bitcast.8.live, bf16[24,256,256]{2,1,0:T(8,128)(2,1)} %bitcast.9, f32[16,128]{1,0:T(8,128)} %bitcast.12, f32[128,128]{1,0:T(8,128)} %bitcast.10), custom_call_target="tpu_custom_call" | custom-call | tf_op jit(solution)/shard_map/pallas_call | solution.py:322
  42.3 2.7 %shard_map.78 = (f32[16,128]{1,0:T(8,128)}, f32[128,128]{1,0:T(8,128)}) custom-call(f32[8,256]{1,0:T(8,128)} %get-tuple-element.7.source, f32[96,256]{1,0:T(8,128)} %get-tuple-element.8.lse, s32[96,128]{1,0:T(8,128)} %get-tuple-element.9.ids, f32[128,128]{1,0:T(8,128)} %bitcast.11), custom_call_target="tpu_custom_call" | custom-call | tf_op jit(solution)/shard_map/pallas_call | solution.py:358

commit v2 on v1

v2 whole, which is shorter than its diff:
```python
import functools

import jax
import jax.numpy as jnp
from jax import lax
from jax.experimental import pallas as pl
from jax.experimental.pallas import tpu as pltpu
from jax.sharding import PartitionSpec as P

ITERS = 3
NEG = -1e30
LOG2E = 1.4426950408889634
LN2 = 0.6931471805599453
LANES = 128
GROUP = 8
UNROLL = 1
HEAD = 28.0
SCALE = 66.0
MESH = pl.DeviceIdType.MESH


def log2(x):
    return jnp.log(x) * LOG2E


def split_peer(me, k, n):
    if n & (n - 1):
        return lax.rem(me + k, n), lax.rem(me + n - k, n)
    other = me
    bit = 1
    while bit <= k:
        if k & bit:
            other = other + bit - 2 * bit * lax.rem(lax.div(me, bit), 2)
        bit *= 2
    return other, other


def kernel(
    n_rows, n_cols,
    brows, bcols, live, costs, log_src, log_tgt,
    src_out, sums_out, into_out, offset_out,
    tiles, tiles_s, tiles_t, rid, cid, base, slot_tot, part_src, src_row, columns, anchor, weight, lt_piece, names, order,
    cid_all, src_buf, tgt_buf,
    load_sem, cid_send, cid_recv, src_send, src_recv, tgt_send, tgt_recv,
):
    slots, bs, _ = tiles.shape
    halves = bs // LANES
    row_blocks = src_row.shape[0]
    my_r = lax.axis_index("rows")
    my_c = lax.axis_index("cols")

    barrier = pltpu.get_barrier_semaphore()
    for k in range(n_cols - 1, 0, -1):
        pl.semaphore_signal(barrier, inc=1, device_id=(my_r, split_peer(my_c, k, n_cols)[0]), device_id_type=MESH)
    for k in range(n_rows - 1, 0, -1):
        pl.semaphore_signal(barrier, inc=1, device_id=(split_peer(my_r, k, n_rows)[0], my_c), device_id_type=MESH)

    loads = []
    for c in range(slots // GROUP):
        part = pl.ds(c * GROUP, GROUP)
        loads.append(pltpu.make_async_copy(costs.at[part], tiles.at[part], load_sem.at[c]))
        loads[-1].start()

    count = live[0]
    for t in range(slots):
        okay = t < count
        rid[t : t + 1, :] = jnp.full((1, bs), jnp.where(okay, brows[t], -1), jnp.int32)
        cid[t : t + 1, :] = jnp.full((1, bs), jnp.where(okay, bcols[t], -1), jnp.int32)
    cid_all[0] = cid[:, :LANES]

    def remote(along, k, src, dst, send_sem, recv_sem):
        if along == "rows":
            peer = (split_peer(my_r, k, n_rows)[0], my_c)
        else:
            peer = (my_r, split_peer(my_c, k, n_cols)[0])
        return pltpu.make_async_remote_copy(
            src_ref=src, dst_ref=dst, send_sem=send_sem.at[k], recv_sem=recv_sem.at[k],
            device_id=peer, device_id_type=MESH)

    def start(copies):
        for copy in copies:
            copy.start()
        return copies

    def as_column(row):
        return jnp.concatenate(
            [jnp.broadcast_to(row[:, h * LANES : (h + 1) * LANES], (LANES, LANES)).T for h in range(halves)], axis=0)

    def groups(body):
        def step(g, _):
            body(g, pl.ds(pl.multiple_of(g * GROUP, GROUP), GROUP))
            return 0

        lax.fori_loop(0, slots // GROUP, step, 0, unroll=UNROLL)

    cuts = [slice(h * LANES, (h + 1) * LANES) for h in range(halves)]
    eye = (lax.broadcasted_iota(jnp.int32, (bs, bs), 0) == lax.broadcasted_iota(jnp.int32, (bs, bs), 1))
    eye = eye.astype(jnp.float32).astype(jnp.bfloat16)
    for c in range(slots // GROUP):
        loads[c].wait()

        at = slice(c * GROUP, (c + 1) * GROUP)
        for lanes in cuts:
            lows, tots = [], []
            for t in range(c * GROUP, (c + 1) * GROUP):
                turned = lax.dot_general(
                    eye, tiles[t, lanes, :], (((1,), (1,)), ((), ())), preferred_element_type=jnp.float32)
                cost = turned * LOG2E
                tiles_t[t, :, lanes] = cost
                low = jnp.min(cost, axis=0, keepdims=True)
                lows.append(low)
                tots.append(jnp.sum(jnp.exp2(low - cost), axis=0, keepdims=True))
            base[at, lanes] = -jnp.concatenate(lows, axis=0)
            slot_tot[at, lanes] = jnp.concatenate(tots, axis=0)

    block_of = lax.broadcasted_iota(jnp.int32, (row_blocks, bs), 0)
    found = base[...] + log2(slot_tot[...])
    masked = [jnp.where(block_of == rid[t : t + 1, :], found[t : t + 1, :], NEG) for t in range(slots)]
    top = functools.reduce(jnp.maximum, masked)
    total = functools.reduce(jnp.add, [jnp.exp2(value - top) for value in masked])
    part_src[0] = top + log2(total)
    src_buf[0, pl.ds(my_c, 1)] = part_src[0][None]

    pl.semaphore_wait(barrier, n_rows + n_cols - 2)

    def send_src(sweep):
        return start([
            remote("cols", k, part_src.at[sweep], src_buf.at[sweep, my_c], src_send.at[sweep], src_recv.at[sweep])
            for k in range(n_cols - 1, 0, -1)])

    def get_src(sweep):
        for k in range(1, n_cols):
            frm = split_peer(my_c, k, n_cols)[1]
            remote("cols", k, part_src.at[sweep], src_buf.at[sweep, frm], src_send.at[sweep], src_recv.at[sweep]).wait_recv()
        return [src_buf[sweep, k] for k in range(n_cols)]

    def tgt_copy(sweep, k):
        return remote("rows", k, tgt_buf.at[sweep, 0], tgt_buf.at[sweep, k], tgt_send.at[sweep], tgt_recv.at[sweep])

    def send_tgt(sweep):
        return start([tgt_copy(sweep, k) for k in range(n_rows - 1, 0, -1)])

    def cid_copy(k):
        return remote("rows", k, cid_all.at[0], cid_all.at[k], cid_send, cid_recv)

    waits = send_src(0)
    waits += start([cid_copy(k) for k in range(n_rows - 1, 0, -1)])

    def natural(g, at):
        for i in range(GROUP):
            tiles_s[g * GROUP + i] = tiles[g * GROUP + i].astype(jnp.float32) * LOG2E

    groups(natural)

    for t in range(slots):
        col_at = bcols[t] * halves
        for h, lanes in enumerate(cuts):
            lt_piece[t : t + 1, lanes] = log_tgt[pl.ds(col_at + h, 1), :] * LOG2E
    log_a = jnp.concatenate([log_src[pl.ds(h, row_blocks, stride=halves), :] for h in range(halves)], axis=1) * LOG2E

    theirs = get_src(0)
    top = functools.reduce(jnp.maximum, theirs)
    total = functools.reduce(jnp.add, [jnp.exp2(value - top) for value in theirs])
    first = log_a - (top + log2(total))
    src_row[...] = first

    def put_columns(values):
        for b in range(row_blocks):
            columns[b] = as_column(values[b : b + 1, :])

    put_columns(first)

    def first_col(g, at):
        for lanes in cuts:
            tops, tots = [], []
            for i in range(GROUP):
                t = g * GROUP + i
                score = columns[brows[t]] - tiles_s[t, :, lanes]
                top = jnp.max(score, axis=0, keepdims=True) - HEAD
                entry = jnp.exp2(score - top)
                tiles_s[t, :, lanes] = entry
                tops.append(top)
                tots.append(jnp.sum(entry, axis=0, keepdims=True))
            base[at, lanes] = jnp.concatenate(tops, axis=0)
            slot_tot[at, lanes] = jnp.concatenate(tots, axis=0)

    groups(first_col)
    alive = cid[...] >= 0
    tgt_buf[0, 0] = jnp.where(alive, base[...] + log2(slot_tot[...]), NEG)
    waits += send_tgt(0)

    def first_turned(g, at):
        bases = base[at, :]
        for i in range(GROUP):
            t = g * GROUP + i
            down = as_column(bases[i : i + 1])
            row = src_row[pl.ds(brows[t], 1), :]
            for lanes in cuts:
                tiles_t[t, :, lanes] = jnp.exp2((row[:, lanes] - tiles_t[t, :, lanes]) - down)

    groups(first_turned)
    for k in range(1, n_rows):
        cid_copy(k).wait_recv()

    def wide(mask):
        return jnp.concatenate([mask] * halves, axis=1)

    def fold(sweep, k, op, so_far, fill):
        ids = cid[:, :LANES]

        def body(g, so_far):
            at = pl.ds(pl.multiple_of(g * GROUP, GROUP), GROUP)
            theirs, values = cid_all[k, at, :], tgt_buf[sweep, k, at, :]
            for i in range(GROUP):
                so_far = op(so_far, jnp.where(wide(ids == theirs[i : i + 1]), values[i : i + 1], fill))
            return so_far

        return lax.fori_loop(0, slots // GROUP, body, so_far, unroll=n_rows <= 4)

    top = jnp.full((slots, bs), NEG, jnp.float32)
    for k in range(n_rows):
        if k:
            tgt_copy(0, k).wait_recv()
        top = fold(0, k, jnp.maximum, top, NEG)
    total = jnp.zeros((slots, bs), jnp.float32)
    for k in range(n_rows):
        total = fold(0, k, lambda so_far, value: so_far + jnp.exp2(value - top), total, NEG)
    gain = lt_piece[...] - (top + log2(total)) + (base[...] + SCALE)
    anchor[...] = jnp.where(alive, jnp.exp2(gain), 0.0)
    weight[...] = anchor[...]
    goal_a = jnp.exp2(log_a + SCALE)

    def dense():
        blocks = offset_out.shape[0]
        padded = sums_out.shape[0]
        if padded > n_rows * slots:
            names[n_rows * slots :, :] = jnp.full((padded - n_rows * slots, LANES), -2.0, jnp.float32)
        for k in range(n_rows):
            frm = split_peer(my_r, k, n_rows)[1]
            names[pl.ds(pl.multiple_of(frm * slots, GROUP), slots), :] = cid_all[k].astype(jnp.float32)
            order[pl.ds(pl.multiple_of(frm * slots, GROUP), slots), :] = tgt_buf[0, k]
        for j in range(padded // LANES):
            line = names[j * LANES : (j + 1) * LANES, :].T[0:1, :]
            into_out[:, j * LANES : (j + 1) * LANES] = jnp.where(
                line == lax.broadcasted_iota(jnp.int32, (blocks, LANES), 0).astype(jnp.float32), 1.0, 0.0)
        per = 16 if blocks % 16 == 0 else blocks
        for b in range(0, blocks, per):
            block = (lax.broadcasted_iota(jnp.int32, (per, LANES), 0) + b).astype(jnp.float32)

            def walk(op, start):
                def body(g, so_far):
                    at = pl.ds(pl.multiple_of(g * GROUP, GROUP), GROUP)
                    theirs, values = names[at, :], order[at, :]
                    for i in range(GROUP):
                        so_far = op(so_far, jnp.where(wide(block == theirs[i : i + 1]), values[i : i + 1], NEG))
                    return so_far

                return lax.fori_loop(0, n_rows * slots // GROUP, body, start)

            top = walk(jnp.maximum, jnp.full((per, bs), NEG, jnp.float32))
            total = walk(lambda so_far, value: so_far + jnp.exp2(value - top), jnp.zeros((per, bs), jnp.float32))
            goal = jnp.concatenate(
                [log_tgt[pl.ds(b * halves + h, per, stride=halves), :] for h in range(halves)], axis=1) * LOG2E
            offset_out[b : b + per, :] = goal - (top + log2(total)) + (goal + SCALE)

    for sweep in range(1, ITERS):
        def row_sums(g, at):
            rows = weight[at, :]
            sums = []
            for i in range(GROUP):
                t = g * GROUP + i
                down = as_column(rows[i : i + 1])
                sums.append(jnp.concatenate(
                    [jnp.sum(tiles_t[t, :, lanes] * down, axis=0, keepdims=True) for lanes in cuts], axis=1))
            slot_tot[at, :] = jnp.concatenate(sums, axis=0)

        groups(row_sums)
        part_src[sweep] = functools.reduce(
            jnp.add, [jnp.where(block_of == rid[t : t + 1, :], slot_tot[t : t + 1, :], 0.0) for t in range(slots)])
        src_buf[sweep, pl.ds(my_c, 1)] = part_src[sweep][None]
        waits += send_src(sweep)
        if sweep == 1:
            dense()
        scaling = goal_a / functools.reduce(jnp.add, get_src(sweep))
        put_columns(scaling)

        def col_sums(g, at):
            sums = []
            for i in range(GROUP):
                t = g * GROUP + i
                down = columns[brows[t]]
                sums.append(jnp.concatenate(
                    [jnp.sum(tiles_s[t, :, lanes] * down, axis=0, keepdims=True) for lanes in cuts], axis=1))
            slot_tot[at, :] = jnp.concatenate(sums, axis=0)

        groups(col_sums)
        tgt_buf[sweep, 0] = anchor[...] * slot_tot[...]
        waits += send_tgt(sweep)
        if sweep == ITERS - 1:
            src_out[...] = (src_row[...] + log2(scaling)) * LN2
            if sums_out.shape[0] > n_rows * slots:
                sums_out[n_rows * slots :, :] = jnp.zeros((sums_out.shape[0] - n_rows * slots, bs), jnp.float32)
            for k in range(n_rows):
                if k:
                    tgt_copy(sweep, k).wait_recv()
                frm = split_peer(my_r, k, n_rows)[1]
                sums_out[pl.ds(pl.multiple_of(frm * slots, GROUP), slots), :] = tgt_buf[sweep, k]
            continue
        goal_b = jnp.exp2(lt_piece[...] + SCALE)
        total = jnp.zeros((slots, bs), jnp.float32)
        for k in range(n_rows):
            if k:
                tgt_copy(sweep, k).wait_recv()
            total = fold(sweep, k, jnp.add, total, 0.0)
        weight[...] = jnp.where(alive, anchor[...] * (goal_b / total), 0.0)
    for copy in waits:
        copy.wait_send()


def final_kernel(source, sums, into, offset, src_out, tgt_out):
    blocks, bs = offset.shape
    halves = bs // LANES
    pick = into[...].astype(jnp.bfloat16)
    rest = sums[...]
    total = None
    for _ in range(3):
        part = rest.astype(jnp.bfloat16)
        rest = rest - part.astype(jnp.float32)
        here = jnp.dot(pick, part, preferred_element_type=jnp.float32)
        total = here if total is None else total + here
    target = (offset[...] - log2(total)) * LN2
    for h in range(halves):
        tgt_out[pl.ds(h, blocks, stride=halves), :] = target[:, h * LANES : (h + 1) * LANES]
        src_out[pl.ds(h, source.shape[0], stride=halves), :] = source[:, h * LANES : (h + 1) * LANES]


def per_device(n_rows, n_cols, costs, block_rows, block_cols, live, log_source, log_target):
    tiles = costs[0, 0]
    slots, bs, _ = tiles.shape
    src_rows = log_source.shape[0] // LANES
    tgt_rows = log_target.shape[0] // LANES
    row_blocks = log_source.shape[0] // bs
    f32 = jnp.float32
    halves = bs // LANES
    dma = pltpu.SemaphoreType.DMA
    smem = pl.BlockSpec(memory_space=pltpu.SMEM)
    vmem = pl.BlockSpec(memory_space=pltpu.VMEM)
    found = pl.cdiv(n_rows * slots, LANES) * LANES
    blocks = log_target.shape[0] // bs
    source, sums, into, offset = pl.pallas_call(
        functools.partial(kernel, n_rows, n_cols),
        out_shape=(
            jax.ShapeDtypeStruct((row_blocks, bs), f32),
            jax.ShapeDtypeStruct((found, bs), f32),
            jax.ShapeDtypeStruct((blocks, found), f32),
            jax.ShapeDtypeStruct((blocks, bs), f32),
        ),
        in_specs=[smem, smem, smem, pl.BlockSpec(memory_space=pl.ANY), vmem, vmem],
        out_specs=(vmem, vmem, vmem, vmem),
        scratch_shapes=[
            pltpu.VMEM((slots, bs, bs), tiles.dtype),
            pltpu.VMEM((slots, bs, bs), f32),
            pltpu.VMEM((slots, bs, bs), f32),
            pltpu.VMEM((slots, bs), jnp.int32),
            pltpu.VMEM((slots, bs), jnp.int32),
            pltpu.VMEM((slots, bs), f32),
            pltpu.VMEM((slots, bs), f32),
            pltpu.VMEM((ITERS, row_blocks, bs), f32),
            pltpu.VMEM((row_blocks, bs), f32),
            pltpu.VMEM((row_blocks, bs, LANES), f32),
            pltpu.VMEM((slots, bs), f32),
            pltpu.VMEM((slots, bs), f32),
            pltpu.VMEM((slots, bs), f32),
            pltpu.VMEM((found, LANES), f32),
            pltpu.VMEM((found, bs), f32),
            pltpu.VMEM((n_rows, slots, LANES), jnp.int32),
            pltpu.VMEM((ITERS, n_cols, row_blocks, bs), f32),
            pltpu.VMEM((ITERS, n_rows, slots, bs), f32),
            dma((slots // GROUP,)),
            dma((n_rows,)), dma((n_rows,)),
            dma((ITERS, n_cols)), dma((ITERS, n_cols)),
            dma((ITERS, n_rows)), dma((ITERS, n_rows)),
        ],
        compiler_params=pltpu.CompilerParams(collective_id=0, has_side_effects=True),
    )(
        block_rows.reshape(-1), block_cols.reshape(-1), live.reshape(-1), tiles,
        log_source.reshape(src_rows, LANES), log_target.reshape(tgt_rows, LANES),
    )
    source, target = pl.pallas_call(
        final_kernel,
        out_shape=(jax.ShapeDtypeStruct((src_rows, LANES), f32), jax.ShapeDtypeStruct((tgt_rows, LANES), f32)),
        in_specs=[vmem] * 4,
        out_specs=(vmem, vmem),
    )(source, sums, into, offset)
    return source.reshape(-1), target.reshape(-1)


def solution(mesh):
    in_specs = (
        P("rows", "cols", None, None, None),
        P("rows", "cols", None),
        P("rows", "cols", None),
        P("rows", "cols"),
        P("rows"),
        P("cols"),
    )
    out_specs = (P("rows"), P("cols"))
    body = functools.partial(per_device, mesh.shape["rows"], mesh.shape["cols"])
    return jax.shard_map(body, mesh=mesh, in_specs=in_specs, out_specs=out_specs, check_vma=False)
```

time: 45.2 us -> 41.2 us (0.912)
  Pallas kernels: 43.7 us -> 39.7 us
    pallas_call x1, Pallas kernels: 41 us -> 38 us  [per_device(): pl.pallas_call(functools.partial(kernel, n_rows, n_cols), out_shape=(jax....]
    pallas_call x1, Pallas kernels: 2.68 us -> 1.75 us  [per_device(): pl.pallas_call(final_kernel, out_shape=(jax.ShapeDtypeStruct((src_rows, L...]
where the time goes in v2:
time: 41.2 us; the launch traced here: 41 us
  Pallas kernels  39.7 us (96%)
  between operations  1.28 us (3%)
    pallas_call x1, Pallas kernels, per_device(): pl.pallas_call(functools.partial(kernel, n_rows, n_cols), out_shape=(jax....  38 us
    pallas_call x1, Pallas kernels, per_device(): pl.pallas_call(final_kernel, out_shape=(jax.ShapeDtypeStruct((src_rows, L...  1.75 us

profile of v2, /device:TPU:0, one launch (start us, length us, event | category | flops | bytes accessed | tf_op | source)
XLA Modules:
  0.0 41.0 jit_solution(1407374594450453519)
XLA Ops:
  1.3 38.0 %shard_map.77 = (f32[8,256]{1,0:T(8,128)}, f32[128,256]{1,0:T(8,128)}, f32[64,128]{1,0:T(8,128)}, f32[64,256]{1,0:T(8,128)}) custom-call(s32[24]{0:T(128)} %bitcast.12, s32[24]{0:T(128)} %bitcast.13, s32[1]{0:T(128)} %bitcast.8.live, bf16[24,256,256]{2,1,0:T(8,128)(2,1)} %bitcast.9, f32[16,128]{1,0:T(8,128)} %bitcast.11, f32[128,128]{1,0:T(8,128)} %bitcast.10), custom_call_target="tpu_custom_call" | custom-call | tf_op jit(solution)/shard_map/pallas_call | solution.py:350
  39.3 1.8 %shard_map.78 = (f32[16,128]{1,0:T(8,128)}, f32[128,128]{1,0:T(8,128)}) custom-call(f32[8,256]{1,0:T(8,128)} %get-tuple-element.8.source, f32[128,256]{1,0:T(8,128)} %get-tuple-element.9.sums, f32[64,128]{1,0:T(8,128)} %get-tuple-element.10.into, f32[64,256]{1,0:T(8,128)} %get-tuple-element.11.offset), custom_call_target="tpu_custom_call" | custom-call | tf_op jit(solution)/shard_map/pallas_call | solution.py:389

commit v3 on v2

--- a/solution.py
+++ b/solution.py
@@ -13,7 +13,7 @@
 LN2 = 0.6931471805599453
 LANES = 128
 GROUP = 8
-UNROLL = 1
+UNROLL = True
 HEAD = 28.0
 SCALE = 66.0
 MESH = pl.DeviceIdType.MESH
@@ -35,11 +35,15 @@
     return other, other
 
 
+def far_first(n):
+    return sorted(range(1, n), key=lambda k: (-(k // 2), k % 2))
+
+
 def kernel(
     n_rows, n_cols,
     brows, bcols, live, costs, log_src, log_tgt,
     src_out, sums_out, into_out, offset_out,
-    tiles, tiles_s, tiles_t, rid, cid, base, slot_tot, part_src, src_row, columns, anchor, weight, lt_piece, names, order,
+    tiles, tiles_s, tiles_t, rid, cid, base, slot_tot, part_src, src_row, columns, anchor, weight, lt_piece, names, order, pick,
     cid_all, src_buf, tgt_buf,
     load_sem, cid_send, cid_recv, src_send, src_recv, tgt_send, tgt_recv,
 ):
@@ -52,7 +56,7 @@
     barrier = pltpu.get_barrier_semaphore()
     for k in range(n_cols - 1, 0, -1):
         pl.semaphore_signal(barrier, inc=1, device_id=(my_r, split_peer(my_c, k, n_cols)[0]), device_id_type=MESH)
-    for k in range(n_rows - 1, 0, -1):
+    for k in far_first(n_rows):
         pl.semaphore_signal(barrier, inc=1, device_id=(split_peer(my_r, k, n_rows)[0], my_c), device_id_type=MESH)
 
     loads = []
@@ -85,6 +89,21 @@
     def as_column(row):
         return jnp.concatenate(
             [jnp.broadcast_to(row[:, h * LANES : (h + 1) * LANES], (LANES, LANES)).T for h in range(halves)], axis=0)
+
+    def turned_parts(values):
+        parts, rest = [], values
+        for _ in range(3):
+            part = rest.astype(jnp.bfloat16).astype(jnp.float32)
+            rest = rest - part
+            parts.append(part)
+            if slots > values.shape[0]:
+                parts.append(jnp.zeros((slots - values.shape[0], bs), jnp.float32))
+        parts.append(jnp.zeros((LANES - 3 * slots, bs), jnp.float32))
+        stack = jnp.concatenate(parts, axis=0)
+        return jnp.concatenate([stack[:, lanes].T for lanes in cuts], axis=0).astype(jnp.bfloat16)
+
+    def spread(turned, t):
+        return lax.dot_general(turned, pick[t], (((1,), (0,)), ((), ())), preferred_element_type=jnp.float32)
 
     def groups(body):
         def step(g, _):
@@ -138,16 +157,21 @@
         return remote("rows", k, tgt_buf.at[sweep, 0], tgt_buf.at[sweep, k], tgt_send.at[sweep], tgt_recv.at[sweep])
 
     def send_tgt(sweep):
-        return start([tgt_copy(sweep, k) for k in range(n_rows - 1, 0, -1)])
+        return start([tgt_copy(sweep, k) for k in far_first(n_rows)])
 
     def cid_copy(k):
         return remote("rows", k, cid_all.at[0], cid_all.at[k], cid_send, cid_recv)
 
     waits = send_src(0)
-    waits += start([cid_copy(k) for k in range(n_rows - 1, 0, -1)])
+    waits += start([cid_copy(k) for k in far_first(n_rows)])
+
+    line = lax.rem(lax.broadcasted_iota(jnp.int32, (LANES, LANES), 0), slots)
+    inside = lax.broadcasted_iota(jnp.int32, (LANES, LANES), 0) < 3 * slots
 
     def natural(g, at):
         for i in range(GROUP):
+            here = jnp.where(inside & (line == g * GROUP + i), 1.0, 0.0)
+            pick[g * GROUP + i] = here.astype(jnp.bfloat16)
             tiles_s[g * GROUP + i] = tiles[g * GROUP + i].astype(jnp.float32) * LOG2E
 
     groups(natural)
@@ -165,8 +189,9 @@
     src_row[...] = first
 
     def put_columns(values):
+        turned = turned_parts(values)
         for b in range(row_blocks):
-            columns[b] = as_column(values[b : b + 1, :])
+            columns[b] = spread(turned, b) if b % 2 else as_column(values[b : b + 1, :])
 
     put_columns(first)
 
@@ -264,12 +289,14 @@
             offset_out[b : b + per, :] = goal - (top + log2(total)) + (goal + SCALE)
 
     for sweep in range(1, ITERS):
+        turned = turned_parts(weight[...])
+
         def row_sums(g, at):
             rows = weight[at, :]
             sums = []
             for i in range(GROUP):
                 t = g * GROUP + i
-                down = as_column(rows[i : i + 1])
+                down = spread(turned, t) if i % 2 else as_column(rows[i : i + 1])
                 sums.append(jnp.concatenate(
                     [jnp.sum(tiles_t[t, :, lanes] * down, axis=0, keepdims=True) for lanes in cuts], axis=1))
             slot_tot[at, :] = jnp.concatenate(sums, axis=0)
@@ -373,6 +400,7 @@
             pltpu.VMEM((slots, bs), f32),
             pltpu.VMEM((found, LANES), f32),
             pltpu.VMEM((found, bs), f32),
+            pltpu.VMEM((slots, LANES, LANES), jnp.bfloat16),
             pltpu.VMEM((n_rows, slots, LANES), jnp.int32),
             pltpu.VMEM((ITERS, n_cols, row_blocks, bs), f32),
             pltpu.VMEM((ITERS, n_rows, slots, bs), f32),

time: 41.2 us -> 40 us (0.971)
  Pallas kernels: 39.7 us -> 38.5 us
    pallas_call x1, Pallas kernels: 38 us -> 36.8 us  [per_device(): pl.pallas_call(functools.partial(kernel, n_rows, n_cols), out_shape=(jax....]
where the time goes in v3:
time: 40 us; the launch traced here: 39.8 us
  Pallas kernels  38.5 us (96%)
  between operations  1.28 us (3%)
    pallas_call x1, Pallas kernels, per_device(): pl.pallas_call(functools.partial(kernel, n_rows, n_cols), out_shape=(jax....  36.8 us
    pallas_call x1, Pallas kernels, per_device(): pl.pallas_call(final_kernel, out_shape=(jax.ShapeDtypeStruct((src_rows, L...  1.75 us

profile of v3, /device:TPU:0, one launch (start us, length us, event | category | flops | bytes accessed | tf_op | source)
XLA Modules:
  0.0 39.8 jit_solution(13961753390006642240)
XLA Ops:
  1.3 36.8 %shard_map.77 = (f32[8,256]{1,0:T(8,128)}, f32[128,256]{1,0:T(8,128)}, f32[64,128]{1,0:T(8,128)}, f32[64,256]{1,0:T(8,128)}) custom-call(s32[24]{0:T(128)} %bitcast.12, s32[24]{0:T(128)} %bitcast.13, s32[1]{0:T(128)} %bitcast.8.live, bf16[24,256,256]{2,1,0:T(8,128)(2,1)} %bitcast.9, f32[16,128]{1,0:T(8,128)} %bitcast.11, f32[128,128]{1,0:T(8,128)} %bitcast.10), custom_call_target="tpu_custom_call" | custom-call | tf_op jit(solution)/shard_map/pallas_call | solution.py:377
  38.1 1.8 %shard_map.78 = (f32[16,128]{1,0:T(8,128)}, f32[128,128]{1,0:T(8,128)}) custom-call(f32[8,256]{1,0:T(8,128)} %get-tuple-element.8.source, f32[128,256]{1,0:T(8,128)} %get-tuple-element.9.sums, f32[64,128]{1,0:T(8,128)} %get-tuple-element.10.into, f32[64,256]{1,0:T(8,128)} %get-tuple-element.11.offset), custom_call_target="tpu_custom_call" | custom-call | tf_op jit(solution)/shard_map/pallas_call | solution.py:417
